TPU v7x, 32 devices: a whole 2x2x4 slice. The times are simulated.
32 devices in a mesh: lon: 8 (over z, y), lat: 4 (over x, core).
Axes of the slice: x: 2, y: 2, z: 4, core: 2. Of those that a mesh axis runs over, the one named last changes fastest.
Arguments:
- zonal_velocity: float32 [40, 64, 1024], P(None, 'lat', 'lon'), as said below
- northward_velocity: float32 [40, 64, 1024], P(None, 'lat', 'lon'), as said below
- level_count: int32 [64, 1024], P('lat', 'lon'), may hold values from 0 to 40, as said below
- surface_height: float32 [64, 1024], P('lat', 'lon'), may hold values from -4 to 4
- zonal_transport: float32 [64, 1024], P('lat', 'lon'), may hold values from -4 to 4
- northward_transport: float32 [64, 1024], P('lat', 'lon'), may hold values from -4 to 4
- thickness: float32 [40], replicated, may hold values from 0.015 to 0.06
Outputs:
- zonal_after: float32 [40, 64, 1024], P(None, 'lat', 'lon')
- northward_after: float32 [40, 64, 1024], P(None, 'lat', 'lon')
- surface_after: float32 [64, 1024], P('lat', 'lon')
- zonal_mean: float32 [64, 1024], P('lat', 'lon')
- northward_mean: float32 [64, 1024], P('lat', 'lon')
Inputs may be any that keep to these rules, and one draw needn't show every extreme that they name: `level_count`: ocean cells have 4 to 40 levels and land cells 0; the first and the last latitude rows are land. `zonal_velocity`: zero at every level k (counted from 0) with k >= min(level_count of the cell, level_count of its eastern neighbour), longitude wrapping. `northward_velocity`: zero at every level k (counted from 0) with k >= min(level_count of the cell, level_count of its northern neighbour), latitude wrapping.
All inputs are finite; a program needn't handle non-finite values.
Results may differ from a plain program's by a relative error of at most 0.0003.
Values sent between devices are 32-bit elements; how exact they have to be, the bound alone decides.
A program may use at most 64 MiB of HBM per device.

v0:
```python
import jax
import jax.numpy as jnp
from jax import lax
from jax.sharding import PartitionSpec as P

NSUB = 30


viscosity = 0.01
timestep = 0.35


def padded_2(x, sides, width):
    for axis, dim in sides:
        size, length = (lax.axis_size(axis), x.shape[dim])
        up = [(i, (i + 1) % size) for i in range(size)]
        down = [(j, i) for i, j in up]
        last = lax.slice_in_dim(x, length - width, length, axis=dim)
        first = lax.slice_in_dim(x, 0, width, axis=dim)
        before = lax.ppermute(last, axis, up)
        after = lax.ppermute(first, axis, down)
        x = jnp.concatenate([before, x, after], axis=dim)
    return x


def inner_laplace(grid_field):
    return (
        grid_field[..., 1:-1, 2:]
        + grid_field[..., 1:-1, :-2]
        + grid_field[..., 2:, 1:-1]
        + grid_field[..., :-2, 1:-1]
        - 4.0 * grid_field[..., 1:-1, 1:-1]
    )


def substep(height, flux_east, flux_north, depth_east, depth_north, force_east, force_north):
    spread = flux_east - jnp.roll(flux_east, 1, -1) + flux_north - jnp.roll(flux_north, 1, -2)
    height = height - timestep * spread
    flux_east = (
        flux_east
        - timestep * depth_east * (jnp.roll(height, -1, -1) - height)
        + timestep * force_east
    )
    flux_north = (
        flux_north
        - timestep * depth_north * (jnp.roll(height, -1, -2) - height)
        + timestep * force_north
    )
    return (height, flux_east, flux_north)


def shards(
    zonal_velocity,
    northward_velocity,
    level_count,
    surface_height,
    zonal_transport,
    northward_transport,
    thickness,
):
    layers = thickness.shape[0]
    levels = jnp.arange(layers, dtype=jnp.float32)[:, None, None]
    counts = level_count.astype(jnp.float32)
    stacked = jnp.concatenate([zonal_velocity, northward_velocity, counts[None]], 0)
    padded = padded_2(stacked, (("lon", 2), ("lat", 1)), 2)
    centre = padded[2 * layers, 1:-1, 1:-1]
    count_east = jnp.minimum(centre, padded[2 * layers, 1:-1, 2:])
    count_north = jnp.minimum(centre, padded[2 * layers, 2:, 1:-1])
    wide_east = (levels < count_east).astype(jnp.float32)
    wide_north = (levels < count_north).astype(jnp.float32)
    first_east = wide_east * inner_laplace(padded[:layers])
    first_north = wide_north * inner_laplace(padded[layers : 2 * layers])
    wet_east = wide_east[:, 1:-1, 1:-1]
    wet_north = wide_north[:, 1:-1, 1:-1]
    face_east = count_east[1:-1, 1:-1]
    face_north = count_north[1:-1, 1:-1]
    tend_east = -viscosity * wet_east * inner_laplace(first_east)
    tend_north = -viscosity * wet_north * inner_laplace(first_north)
    layer_depth = thickness[:, None, None]
    depth_east = jnp.sum(layer_depth * wet_east, 0)
    depth_north = jnp.sum(layer_depth * wet_north, 0)
    force_east = jnp.sum(layer_depth * tend_east, 0) / (NSUB * timestep)
    force_north = jnp.sum(layer_depth * tend_north, 0) / (NSUB * timestep)
    after_east = zonal_velocity + tend_east
    after_north = northward_velocity + tend_north
    column_east = jnp.sum(layer_depth * after_east, 0)
    column_north = jnp.sum(layer_depth * after_north, 0)
    open_east = (face_east > 0).astype(jnp.float32)
    open_north = (face_north > 0).astype(jnp.float32)
    statics = jnp.stack([depth_east, depth_north, force_east, force_north])
    margin = 5
    padded_static = padded_2(statics, (("lon", 2), ("lat", 1)), 5)

    def share_rims(state):
        return padded_2(state, (("lon", 2), ("lat", 1)), 5)

    def round_update(round_index, state_carry):
        height, flux_east, flux_north, total_east, total_north = state_carry
        widened = share_rims(jnp.stack([height, flux_east, flux_north]))
        height_wide, east_wide, north_wide = (widened[0], widened[1], widened[2])
        for repeat in range(margin):
            height_wide, east_wide, north_wide = substep(
                height_wide,
                east_wide,
                north_wide,
                padded_static[0],
                padded_static[1],
                padded_static[2],
                padded_static[3],
            )
            total_east = total_east + east_wide[margin:-margin, margin:-margin]
            total_north = total_north + north_wide[margin:-margin, margin:-margin]
        return (
            height_wide[margin:-margin, margin:-margin],
            east_wide[margin:-margin, margin:-margin],
            north_wide[margin:-margin, margin:-margin],
            total_east,
            total_north,
        )

    zeros = jnp.zeros(surface_height.shape, jnp.float32)
    initial = (
        surface_height,
        open_east * zonal_transport,
        open_north * northward_transport,
        zeros,
        zeros,
    )
    height, flux_east, flux_north, total_east, total_north = lax.fori_loop(
        0, NSUB // margin, round_update, initial
    )
    mean_east = total_east / NSUB
    mean_north = total_north / NSUB
    shift_east = (mean_east - column_east) / (depth_east + 1.0 - open_east)
    shift_north = (mean_north - column_north) / (depth_north + 1.0 - open_north)
    zonal_after = wet_east * (after_east + shift_east)
    northward_after = wet_north * (after_north + shift_north)
    return (zonal_after, northward_after, height, mean_east, mean_north)


def solution(mesh):
    placed = (
        P(None, "lat", "lon"),
        P(None, "lat", "lon"),
        P("lat", "lon"),
        P("lat", "lon"),
        P("lat", "lon"),
        P("lat", "lon"),
        P(),
    )
    return jax.shard_map(
        shards,
        mesh=mesh,
        in_specs=placed,
        out_specs=(
            P(None, "lat", "lon"),
            P(None, "lat", "lon"),
            P("lat", "lon"),
            P("lat", "lon"),
            P("lat", "lon"),
        ),
        check_vma=False,
    )
```

profile of v0, /device:TPU:0, one launch (start us, length us, event | category | flops | bytes accessed | tf_op | source)
XLA Modules:
  0.0 115.5 jit_solution(15732596150183590328)
XLA Ops:
  3.0 6.0 %collective-permute-start.5 = (f32[81,16,2]{0,1,2:T(8,128)S(1)}, f32[81,16,2]{0,1,2:T(8,128)S(1)}, u32[]{:S(2)}, u32[]{:S(2)}) collective-permute-start(f32[81,16,2]{0,1,2:T(8,128)S(1)} %copy.32), channel_id=1, source_target_pairs={{4,0},{8,4},{12,8},{16,12},{20,16},{24,20},{28,24},{0,28},{5,1},{9... | collective-permute-start | bytes 31112 | tf_op jit(solution)/shard_map/ppermute | solution.py:21
  10.9 4.9 %collective-permute-done.4 = f32[81,16,2]{0,1,2:T(8,128)S(1)} collective-permute-done((f32[81,16,2]{0,1,2:T(8,128)S(1)}, f32[81,16,2]{0,1,2:T(8,128)S(1)}, u32[]{:S(2)}, u32[]{:S(2)}) %collective-permute-start.4) | collective-permute-done | bytes 10400 | tf_op jit(solution)/shard_map/ppermute | solution.py:20
  17.4 3.2 %collective-permute-done.7 = f32[81,2,132]{2,1,0:T(2,128)S(1)} collective-permute-done((f32[81,2,132]{2,1,0:T(2,128)S(1)}, f32[81,2,132]{2,1,0:T(2,128)S(1)}, u32[]{:S(2)}, u32[]{:S(2)}) %collective-permute-start.7) | collective-permute-done | bytes 85568 | tf_op jit(solution)/shard_map/ppermute | solution.py:21
  20.6 2.9 %collective-permute-done.6 = f32[81,2,132]{2,1,0:T(2,128)S(1)} collective-permute-done((f32[81,2,132]{2,1,0:T(2,128)S(1)}, f32[81,2,132]{2,1,0:T(2,128)S(1)}, u32[]{:S(2)}, u32[]{:S(2)}) %collective-permute-start.6) | collective-permute-done | bytes 85568 | tf_op jit(solution)/shard_map/ppermute | solution.py:20
  29.8 1.9 %collective-permute-start.8 = (f32[4,16,5]{2,1,0:T(8,128)S(1)}, f32[4,16,5]{2,1,0:T(8,128)S(1)}, u32[]{:S(2)}, u32[]{:S(2)}) collective-permute-start(f32[4,16,5]{2,1,0:T(8,128)S(1)} %get-tuple-element.140), channel_id=1, source_target_pairs={{0,4},{4,8},{8,12},{12,16},{16,20},{20,24},{24,28},{28,0},{1,5},{5... | collective-permute-start | bytes 3848 | tf_op jit(solution)/shard_map/ppermute | solution.py:20
  31.8 1.8 %collective-permute-done.9 = f32[4,16,5]{2,1,0:T(8,128)S(1)} collective-permute-done((f32[4,16,5]{2,1,0:T(8,128)S(1)}, f32[4,16,5]{2,1,0:T(8,128)S(1)}, u32[]{:S(2)}, u32[]{:S(2)}) %collective-permute-start.9) | collective-permute-done | bytes 1312 | tf_op jit(solution)/shard_map/ppermute | solution.py:21
  33.6 2.8 %collective-permute-done.8 = f32[4,16,5]{2,1,0:T(8,128)S(1)} collective-permute-done((f32[4,16,5]{2,1,0:T(8,128)S(1)}, f32[4,16,5]{2,1,0:T(8,128)S(1)}, u32[]{:S(2)}, u32[]{:S(2)}) %collective-permute-start.8) | collective-permute-done | bytes 1312 | tf_op jit(solution)/shard_map/ppermute | solution.py:20
  40.1 73.0 %while.19 = (s32[]{:T(128)}, f32[16,128]{1,0:T(8,128)S(1)}, f32[16,128]{1,0:T(8,128)S(1)}, f32[16,128]{1,0:T(8,128)S(1)}, f32[16,128]{1,0:T(8,128)S(1)}, /*index...) while((s32[]{:T(128)}, f32[16,128]{1,0:T(8,128)S(1)}, ...), condition=%wide.region_5.0_spmd.clone, body=%wide.region_4.0_spmd.clone.sunk | while | flops 489287 | bytes 2026912 | solution.py:129
  40.2 2.0 %collective-permute-start.1 = (f32[3,16,5]{2,1,0:T(8,128)S(1)}, f32[3,16,5]{2,1,0:T(8,128)S(1)}, u32[]{:S(2)}, u32[]{:S(2)}) collective-permute-start(f32[3,16,5]{2,1,0:T(8,128)S(1)} %get-tuple-element.209), channel_id=1, source_target_pairs={{0,4},{4,8},{8,12},{12,16},{16,20},{20,24},{24,28},{28,0},{1,5},{5... | collective-permute-start | bytes 2888 | tf_op jit(solution)/shard_map/while/body/eval_jaxpr/ppermute | solution.py:20
  42.2 1.8 %collective-permute-done = f32[3,16,5]{2,1,0:T(8,128)S(1)} collective-permute-done((f32[3,16,5]{2,1,0:T(8,128)S(1)}, f32[3,16,5]{2,1,0:T(8,128)S(1)}, u32[]{:S(2)}, u32[]{:S(2)}) %collective-permute-start) | collective-permute-done | bytes 992 | tf_op jit(solution)/shard_map/while/body/eval_jaxpr/ppermute | solution.py:21
  44.0 2.8 %collective-permute-done.1 = f32[3,16,5]{2,1,0:T(8,128)S(1)} collective-permute-done((f32[3,16,5]{2,1,0:T(8,128)S(1)}, f32[3,16,5]{2,1,0:T(8,128)S(1)}, u32[]{:S(2)}, u32[]{:S(2)}) %collective-permute-start.1) | collective-permute-done | bytes 992 | tf_op jit(solution)/shard_map/while/body/eval_jaxpr/ppermute | solution.py:20
  52.4 2.0 %collective-permute-start.1 = (f32[3,16,5]{2,1,0:T(8,128)S(1)}, f32[3,16,5]{2,1,0:T(8,128)S(1)}, u32[]{:S(2)}, u32[]{:S(2)}) collective-permute-start(f32[3,16,5]{2,1,0:T(8,128)S(1)} %get-tuple-element.209), channel_id=1, source_target_pairs={{0,4},{4,8},{8,12},{12,16},{16,20},{20,24},{24,28},{28,0},{1,5},{5... | collective-permute-start | bytes 2888 | tf_op jit(solution)/shard_map/while/body/eval_jaxpr/ppermute | solution.py:20
  54.4 1.8 %collective-permute-done = f32[3,16,5]{2,1,0:T(8,128)S(1)} collective-permute-done((f32[3,16,5]{2,1,0:T(8,128)S(1)}, f32[3,16,5]{2,1,0:T(8,128)S(1)}, u32[]{:S(2)}, u32[]{:S(2)}) %collective-permute-start) | collective-permute-done | bytes 992 | tf_op jit(solution)/shard_map/while/body/eval_jaxpr/ppermute | solution.py:21
  56.2 2.8 %collective-permute-done.1 = f32[3,16,5]{2,1,0:T(8,128)S(1)} collective-permute-done((f32[3,16,5]{2,1,0:T(8,128)S(1)}, f32[3,16,5]{2,1,0:T(8,128)S(1)}, u32[]{:S(2)}, u32[]{:S(2)}) %collective-permute-start.1) | collective-permute-done | bytes 992 | tf_op jit(solution)/shard_map/while/body/eval_jaxpr/ppermute | solution.py:20
  64.5 2.0 %collective-permute-start.1 = (f32[3,16,5]{2,1,0:T(8,128)S(1)}, f32[3,16,5]{2,1,0:T(8,128)S(1)}, u32[]{:S(2)}, u32[]{:S(2)}) collective-permute-start(f32[3,16,5]{2,1,0:T(8,128)S(1)} %get-tuple-element.209), channel_id=1, source_target_pairs={{0,4},{4,8},{8,12},{12,16},{16,20},{20,24},{24,28},{28,0},{1,5},{5... | collective-permute-start | bytes 2888 | tf_op jit(solution)/shard_map/while/body/eval_jaxpr/ppermute | solution.py:20
  66.5 1.8 %collective-permute-done = f32[3,16,5]{2,1,0:T(8,128)S(1)} collective-permute-done((f32[3,16,5]{2,1,0:T(8,128)S(1)}, f32[3,16,5]{2,1,0:T(8,128)S(1)}, u32[]{:S(2)}, u32[]{:S(2)}) %collective-permute-start) | collective-permute-done | bytes 992 | tf_op jit(solution)/shard_map/while/body/eval_jaxpr/ppermute | solution.py:21
  68.3 2.8 %collective-permute-done.1 = f32[3,16,5]{2,1,0:T(8,128)S(1)} collective-permute-done((f32[3,16,5]{2,1,0:T(8,128)S(1)}, f32[3,16,5]{2,1,0:T(8,128)S(1)}, u32[]{:S(2)}, u32[]{:S(2)}) %collective-permute-start.1) | collective-permute-done | bytes 992 | tf_op jit(solution)/shard_map/while/body/eval_jaxpr/ppermute | solution.py:20
  76.7 2.0 %collective-permute-start.1 = (f32[3,16,5]{2,1,0:T(8,128)S(1)}, f32[3,16,5]{2,1,0:T(8,128)S(1)}, u32[]{:S(2)}, u32[]{:S(2)}) collective-permute-start(f32[3,16,5]{2,1,0:T(8,128)S(1)} %get-tuple-element.209), channel_id=1, source_target_pairs={{0,4},{4,8},{8,12},{12,16},{16,20},{20,24},{24,28},{28,0},{1,5},{5... | collective-permute-start | bytes 2888 | tf_op jit(solution)/shard_map/while/body/eval_jaxpr/ppermute | solution.py:20
  78.7 1.8 %collective-permute-done = f32[3,16,5]{2,1,0:T(8,128)S(1)} collective-permute-done((f32[3,16,5]{2,1,0:T(8,128)S(1)}, f32[3,16,5]{2,1,0:T(8,128)S(1)}, u32[]{:S(2)}, u32[]{:S(2)}) %collective-permute-start) | collective-permute-done | bytes 992 | tf_op jit(solution)/shard_map/while/body/eval_jaxpr/ppermute | solution.py:21
  80.5 2.8 %collective-permute-done.1 = f32[3,16,5]{2,1,0:T(8,128)S(1)} collective-permute-done((f32[3,16,5]{2,1,0:T(8,128)S(1)}, f32[3,16,5]{2,1,0:T(8,128)S(1)}, u32[]{:S(2)}, u32[]{:S(2)}) %collective-permute-start.1) | collective-permute-done | bytes 992 | tf_op jit(solution)/shard_map/while/body/eval_jaxpr/ppermute | solution.py:20
  88.9 2.0 %collective-permute-start.1 = (f32[3,16,5]{2,1,0:T(8,128)S(1)}, f32[3,16,5]{2,1,0:T(8,128)S(1)}, u32[]{:S(2)}, u32[]{:S(2)}) collective-permute-start(f32[3,16,5]{2,1,0:T(8,128)S(1)} %get-tuple-element.209), channel_id=1, source_target_pairs={{0,4},{4,8},{8,12},{12,16},{16,20},{20,24},{24,28},{28,0},{1,5},{5... | collective-permute-start | bytes 2888 | tf_op jit(solution)/shard_map/while/body/eval_jaxpr/ppermute | solution.py:20
  92.7 2.8 %collective-permute-done.1 = f32[3,16,5]{2,1,0:T(8,128)S(1)} collective-permute-done((f32[3,16,5]{2,1,0:T(8,128)S(1)}, f32[3,16,5]{2,1,0:T(8,128)S(1)}, u32[]{:S(2)}, u32[]{:S(2)}) %collective-permute-start.1) | collective-permute-done | bytes 992 | tf_op jit(solution)/shard_map/while/body/eval_jaxpr/ppermute | solution.py:20
  101.0 2.0 %collective-permute-start.1 = (f32[3,16,5]{2,1,0:T(8,128)S(1)}, f32[3,16,5]{2,1,0:T(8,128)S(1)}, u32[]{:S(2)}, u32[]{:S(2)}) collective-permute-start(f32[3,16,5]{2,1,0:T(8,128)S(1)} %get-tuple-element.209), channel_id=1, source_target_pairs={{0,4},{4,8},{8,12},{12,16},{16,20},{20,24},{24,28},{28,0},{1,5},{5... | collective-permute-start | bytes 2888 | tf_op jit(solution)/shard_map/while/body/eval_jaxpr/ppermute | solution.py:20
  104.9 2.8 %collective-permute-done.1 = f32[3,16,5]{2,1,0:T(8,128)S(1)} collective-permute-done((f32[3,16,5]{2,1,0:T(8,128)S(1)}, f32[3,16,5]{2,1,0:T(8,128)S(1)}, u32[]{:S(2)}, u32[]{:S(2)}) %collective-permute-start.1) | collective-permute-done | bytes 992 | tf_op jit(solution)/shard_map/while/body/eval_jaxpr/ppermute | solution.py:20
  (380 shorter events, 53.9 us)
Async XLA Ops:
  3.0 7.5 %collective-permute-start.5 = (f32[81,16,2]{0,1,2:T(8,128)S(1)}, f32[81,16,2]{0,1,2:T(8,128)S(1)}, u32[]{:S(2)}, u32[]{:S(2)}) collective-permute-start(f32[81,16,2]{0,1,2:T(8,128)S(1)} %copy.32), channel_id=1, source_target_pairs={{4,0},{8,4},{12,8},{16,12},{20,16},{24,20},{28,24},{0,28},{5,1},{9... | collective-permute-start | bytes 31112 | tf_op jit(solution)/shard_map/ppermute | solution.py:21
  9.4 6.4 %collective-permute-start.4 = (f32[81,16,2]{0,1,2:T(8,128)S(1)}, f32[81,16,2]{0,1,2:T(8,128)S(1)}, u32[]{:S(2)}, u32[]{:S(2)}) collective-permute-start(f32[81,16,2]{0,1,2:T(8,128)S(1)} %copy.31), channel_id=1, source_target_pairs={{0,4},{4,8},{8,12},{12,16},{16,20},{20,24},{24,28},{28,0},{1,5},{5... | collective-permute-start | bytes 31112 | tf_op jit(solution)/shard_map/ppermute | solution.py:20
  16.9 3.7 %collective-permute-start.7 = (f32[81,2,132]{2,1,0:T(2,128)S(1)}, f32[81,2,132]{2,1,0:T(2,128)S(1)}, u32[]{:S(2)}, u32[]{:S(2)}) collective-permute-start(f32[81,2,132]{2,1,0:T(2,128)S(1)} %get-tuple-element.135), channel_id=1, source_target_pairs={{1,0},{2,1},{3,2},{0,3},{5,4},{6,5},{7,6},{4,7},{9,8},{10,9},{11,1... | collective-permute-start | bytes 256616 | tf_op jit(solution)/shard_map/ppermute | solution.py:21
  16.9 6.6 %collective-permute-start.6 = (f32[81,2,132]{2,1,0:T(2,128)S(1)}, f32[81,2,132]{2,1,0:T(2,128)S(1)}, u32[]{:S(2)}, u32[]{:S(2)}) collective-permute-start(f32[81,2,132]{2,1,0:T(2,128)S(1)} %get-tuple-element.134), channel_id=1, source_target_pairs={{0,1},{1,2},{2,3},{3,0},{4,5},{5,6},{6,7},{7,4},{8,9},{9,10},{10,1... | collective-permute-start | bytes 256616 | tf_op jit(solution)/shard_map/ppermute | solution.py:20
  29.7 3.9 %collective-permute-start.9 = (f32[4,16,5]{2,1,0:T(8,128)S(1)}, f32[4,16,5]{2,1,0:T(8,128)S(1)}, u32[]{:S(2)}, u32[]{:S(2)}) collective-permute-start(f32[4,16,5]{2,1,0:T(8,128)S(1)} %get-tuple-element.141), channel_id=1, source_target_pairs={{4,0},{8,4},{12,8},{16,12},{20,16},{24,20},{28,24},{0,28},{5,1},{9... | collective-permute-start | bytes 3848 | tf_op jit(solution)/shard_map/ppermute | solution.py:21
  29.8 6.6 %collective-permute-start.8 = (f32[4,16,5]{2,1,0:T(8,128)S(1)}, f32[4,16,5]{2,1,0:T(8,128)S(1)}, u32[]{:S(2)}, u32[]{:S(2)}) collective-permute-start(f32[4,16,5]{2,1,0:T(8,128)S(1)} %get-tuple-element.140), channel_id=1, source_target_pairs={{0,4},{4,8},{8,12},{12,16},{16,20},{20,24},{24,28},{28,0},{1,5},{5... | collective-permute-start | bytes 3848 | tf_op jit(solution)/shard_map/ppermute | solution.py:20
  36.6 3.4 %collective-permute-start.10 = (f32[4,5,138]{2,1,0:T(8,128)S(1)}, f32[4,5,138]{2,1,0:T(8,128)S(1)}, u32[]{:S(2)}, u32[]{:S(2)}) collective-permute-start(f32[4,5,138]{2,1,0:T(8,128)S(1)} %get-tuple-element.138), channel_id=1, source_target_pairs={{0,1},{1,2},{2,3},{3,0},{4,5},{5,6},{6,7},{7,4},{8,9},{9,10},{10,1... | collective-permute-start | bytes 33128 | tf_op jit(solution)/shard_map/ppermute | solution.py:20
  40.2 3.8 %collective-permute-start = (f32[3,16,5]{2,1,0:T(8,128)S(1)}, f32[3,16,5]{2,1,0:T(8,128)S(1)}, u32[]{:S(2)}, u32[]{:S(2)}) collective-permute-start(f32[3,16,5]{2,1,0:T(8,128)S(1)} %get-tuple-element.208), channel_id=1, source_target_pairs={{4,0},{8,4},{12,8},{16,12},{20,16},{24,20},{28,24},{0,28},{5,1},{9... | collective-permute-start | bytes 2888 | tf_op jit(solution)/shard_map/while/body/eval_jaxpr/ppermute | solution.py:21
  40.2 6.6 %collective-permute-start.1 = (f32[3,16,5]{2,1,0:T(8,128)S(1)}, f32[3,16,5]{2,1,0:T(8,128)S(1)}, u32[]{:S(2)}, u32[]{:S(2)}) collective-permute-start(f32[3,16,5]{2,1,0:T(8,128)S(1)} %get-tuple-element.209), channel_id=1, source_target_pairs={{0,4},{4,8},{8,12},{12,16},{16,20},{20,24},{24,28},{28,0},{1,5},{5... | collective-permute-start | bytes 2888 | tf_op jit(solution)/shard_map/while/body/eval_jaxpr/ppermute | solution.py:20
  46.9 3.3 %collective-permute-start.3 = (f32[3,5,138]{2,1,0:T(8,128)S(1)}, f32[3,5,138]{2,1,0:T(8,128)S(1)}, u32[]{:S(2)}, u32[]{:S(2)}) collective-permute-start(f32[3,5,138]{2,1,0:T(8,128)S(1)} %get-tuple-element.211), channel_id=1, source_target_pairs={{0,1},{1,2},{2,3},{3,0},{4,5},{5,6},{6,7},{7,4},{8,9},{9,10},{10,1... | collective-permute-start | bytes 24848 | tf_op jit(solution)/shard_map/while/body/eval_jaxpr/ppermute | solution.py:20
  52.3 3.8 %collective-permute-start = (f32[3,16,5]{2,1,0:T(8,128)S(1)}, f32[3,16,5]{2,1,0:T(8,128)S(1)}, u32[]{:S(2)}, u32[]{:S(2)}) collective-permute-start(f32[3,16,5]{2,1,0:T(8,128)S(1)} %get-tuple-element.208), channel_id=1, source_target_pairs={{4,0},{8,4},{12,8},{16,12},{20,16},{24,20},{28,24},{0,28},{5,1},{9... | collective-permute-start | bytes 2888 | tf_op jit(solution)/shard_map/while/body/eval_jaxpr/ppermute | solution.py:21
  52.4 6.6 %collective-permute-start.1 = (f32[3,16,5]{2,1,0:T(8,128)S(1)}, f32[3,16,5]{2,1,0:T(8,128)S(1)}, u32[]{:S(2)}, u32[]{:S(2)}) collective-permute-start(f32[3,16,5]{2,1,0:T(8,128)S(1)} %get-tuple-element.209), channel_id=1, source_target_pairs={{0,4},{4,8},{8,12},{12,16},{16,20},{20,24},{24,28},{28,0},{1,5},{5... | collective-permute-start | bytes 2888 | tf_op jit(solution)/shard_map/while/body/eval_jaxpr/ppermute | solution.py:20
  59.1 3.3 %collective-permute-start.3 = (f32[3,5,138]{2,1,0:T(8,128)S(1)}, f32[3,5,138]{2,1,0:T(8,128)S(1)}, u32[]{:S(2)}, u32[]{:S(2)}) collective-permute-start(f32[3,5,138]{2,1,0:T(8,128)S(1)} %get-tuple-element.211), channel_id=1, source_target_pairs={{0,1},{1,2},{2,3},{3,0},{4,5},{5,6},{6,7},{7,4},{8,9},{9,10},{10,1... | collective-permute-start | bytes 24848 | tf_op jit(solution)/shard_map/while/body/eval_jaxpr/ppermute | solution.py:20
  64.5 3.8 %collective-permute-start = (f32[3,16,5]{2,1,0:T(8,128)S(1)}, f32[3,16,5]{2,1,0:T(8,128)S(1)}, u32[]{:S(2)}, u32[]{:S(2)}) collective-permute-start(f32[3,16,5]{2,1,0:T(8,128)S(1)} %get-tuple-element.208), channel_id=1, source_target_pairs={{4,0},{8,4},{12,8},{16,12},{20,16},{24,20},{28,24},{0,28},{5,1},{9... | collective-permute-start | bytes 2888 | tf_op jit(solution)/shard_map/while/body/eval_jaxpr/ppermute | solution.py:21
  64.5 6.6 %collective-permute-start.1 = (f32[3,16,5]{2,1,0:T(8,128)S(1)}, f32[3,16,5]{2,1,0:T(8,128)S(1)}, u32[]{:S(2)}, u32[]{:S(2)}) collective-permute-start(f32[3,16,5]{2,1,0:T(8,128)S(1)} %get-tuple-element.209), channel_id=1, source_target_pairs={{0,4},{4,8},{8,12},{12,16},{16,20},{20,24},{24,28},{28,0},{1,5},{5... | collective-permute-start | bytes 2888 | tf_op jit(solution)/shard_map/while/body/eval_jaxpr/ppermute | solution.py:20
  76.7 3.8 %collective-permute-start = (f32[3,16,5]{2,1,0:T(8,128)S(1)}, f32[3,16,5]{2,1,0:T(8,128)S(1)}, u32[]{:S(2)}, u32[]{:S(2)}) collective-permute-start(f32[3,16,5]{2,1,0:T(8,128)S(1)} %get-tuple-element.208), channel_id=1, source_target_pairs={{4,0},{8,4},{12,8},{16,12},{20,16},{24,20},{28,24},{0,28},{5,1},{9... | collective-permute-start | bytes 2888 | tf_op jit(solution)/shard_map/while/body/eval_jaxpr/ppermute | solution.py:21
  76.7 6.6 %collective-permute-start.1 = (f32[3,16,5]{2,1,0:T(8,128)S(1)}, f32[3,16,5]{2,1,0:T(8,128)S(1)}, u32[]{:S(2)}, u32[]{:S(2)}) collective-permute-start(f32[3,16,5]{2,1,0:T(8,128)S(1)} %get-tuple-element.209), channel_id=1, source_target_pairs={{0,4},{4,8},{8,12},{12,16},{16,20},{20,24},{24,28},{28,0},{1,5},{5... | collective-permute-start | bytes 2888 | tf_op jit(solution)/shard_map/while/body/eval_jaxpr/ppermute | solution.py:20
  83.4 3.3 %collective-permute-start.3 = (f32[3,5,138]{2,1,0:T(8,128)S(1)}, f32[3,5,138]{2,1,0:T(8,128)S(1)}, u32[]{:S(2)}, u32[]{:S(2)}) collective-permute-start(f32[3,5,138]{2,1,0:T(8,128)S(1)} %get-tuple-element.211), channel_id=1, source_target_pairs={{0,1},{1,2},{2,3},{3,0},{4,5},{5,6},{6,7},{7,4},{8,9},{9,10},{10,1... | collective-permute-start | bytes 24848 | tf_op jit(solution)/shard_map/while/body/eval_jaxpr/ppermute | solution.py:20
  88.9 3.8 %collective-permute-start = (f32[3,16,5]{2,1,0:T(8,128)S(1)}, f32[3,16,5]{2,1,0:T(8,128)S(1)}, u32[]{:S(2)}, u32[]{:S(2)}) collective-permute-start(f32[3,16,5]{2,1,0:T(8,128)S(1)} %get-tuple-element.208), channel_id=1, source_target_pairs={{4,0},{8,4},{12,8},{16,12},{20,16},{24,20},{28,24},{0,28},{5,1},{9... | collective-permute-start | bytes 2888 | tf_op jit(solution)/shard_map/while/body/eval_jaxpr/ppermute | solution.py:21
  88.9 6.6 %collective-permute-start.1 = (f32[3,16,5]{2,1,0:T(8,128)S(1)}, f32[3,16,5]{2,1,0:T(8,128)S(1)}, u32[]{:S(2)}, u32[]{:S(2)}) collective-permute-start(f32[3,16,5]{2,1,0:T(8,128)S(1)} %get-tuple-element.209), channel_id=1, source_target_pairs={{0,4},{4,8},{8,12},{12,16},{16,20},{20,24},{24,28},{28,0},{1,5},{5... | collective-permute-start | bytes 2888 | tf_op jit(solution)/shard_map/while/body/eval_jaxpr/ppermute | solution.py:20
  95.6 3.3 %collective-permute-start.3 = (f32[3,5,138]{2,1,0:T(8,128)S(1)}, f32[3,5,138]{2,1,0:T(8,128)S(1)}, u32[]{:S(2)}, u32[]{:S(2)}) collective-permute-start(f32[3,5,138]{2,1,0:T(8,128)S(1)} %get-tuple-element.211), channel_id=1, source_target_pairs={{0,1},{1,2},{2,3},{3,0},{4,5},{5,6},{6,7},{7,4},{8,9},{9,10},{10,1... | collective-permute-start | bytes 24848 | tf_op jit(solution)/shard_map/while/body/eval_jaxpr/ppermute | solution.py:20
  101.0 3.8 %collective-permute-start = (f32[3,16,5]{2,1,0:T(8,128)S(1)}, f32[3,16,5]{2,1,0:T(8,128)S(1)}, u32[]{:S(2)}, u32[]{:S(2)}) collective-permute-start(f32[3,16,5]{2,1,0:T(8,128)S(1)} %get-tuple-element.208), channel_id=1, source_target_pairs={{4,0},{8,4},{12,8},{16,12},{20,16},{24,20},{28,24},{0,28},{5,1},{9... | collective-permute-start | bytes 2888 | tf_op jit(solution)/shard_map/while/body/eval_jaxpr/ppermute | solution.py:21
  101.0 6.6 %collective-permute-start.1 = (f32[3,16,5]{2,1,0:T(8,128)S(1)}, f32[3,16,5]{2,1,0:T(8,128)S(1)}, u32[]{:S(2)}, u32[]{:S(2)}) collective-permute-start(f32[3,16,5]{2,1,0:T(8,128)S(1)} %get-tuple-element.209), channel_id=1, source_target_pairs={{0,4},{4,8},{8,12},{12,16},{16,20},{20,24},{24,28},{28,0},{1,5},{5... | collective-permute-start | bytes 2888 | tf_op jit(solution)/shard_map/while/body/eval_jaxpr/ppermute | solution.py:20
  107.8 3.3 %collective-permute-start.3 = (f32[3,5,138]{2,1,0:T(8,128)S(1)}, f32[3,5,138]{2,1,0:T(8,128)S(1)}, u32[]{:S(2)}, u32[]{:S(2)}) collective-permute-start(f32[3,5,138]{2,1,0:T(8,128)S(1)} %get-tuple-element.211), channel_id=1, source_target_pairs={{0,1},{1,2},{2,3},{3,0},{4,5},{5,6},{6,7},{7,4},{8,9},{9,10},{10,1... | collective-permute-start | bytes 24848 | tf_op jit(solution)/shard_map/while/body/eval_jaxpr/ppermute | solution.py:20
  (15 other events, 68.7 us)
where the time goes:
time: 116 us; the launch traced here: 115 us
  waiting for transfers between devices  63.5 us (55%)
  starting transfers between devices  24.7 us (21%)
  other arithmetic  17.9 us (15%)
  local copies, waits for them, and re-layouts  7.23 us (6%)
  loops' own time  1.27 us (1%)
    ppermute x16, waiting for transfers between devices, padded_2(): before = lax.ppermute(last, axis, up)  39.5 us
    ppermute x16, waiting for transfers between devices, padded_2(): after = lax.ppermute(first, axis, down)  24 us
    ppermute x16, starting transfers between devices, padded_2(): before = lax.ppermute(last, axis, up)  18.1 us
    ppermute x16, starting transfers between devices, padded_2(): after = lax.ppermute(first, axis, down)  6.6 us
    concatenate x16, other arithmetic, padded_2(): x = jnp.concatenate([before, x, after], axis=dim)  2.75 us
    sub x30, other arithmetic, substep(): height = height - timestep * spread  2.53 us
  transfers between devices with their start and end apart: 32, of which 32 were waited for; matrix products, arithmetic and copies ran while one was open for 1% of the time, Pallas kernels for 0%

commit v1 on v0

v1 whole, which is shorter than its diff:
```python
import functools

import jax
import jax.numpy as jnp
from jax import lax
from jax.experimental import pallas as pl
from jax.experimental.pallas import tpu as pltpu
from jax.sharding import PartitionSpec as P

NSUB = 30
VISCOSITY = 0.01
TIMESTEP = 0.35
LANES = 128
GROUP = 4
PER_TILE = LANES // GROUP
MESH = pl.DeviceIdType.MESH


def lane_of(x):
    return lax.broadcasted_iota(jnp.int32, x.shape, 1)


def sub_of(x):
    return lax.broadcasted_iota(jnp.int32, x.shape, 0)


def lanes(x, shift):
    return pltpu.roll(x, shift % LANES, 1)


def up(x):
    return pltpu.roll(x, x.shape[0] - 1, 0)


def down(x):
    return pltpu.roll(x, 1, 0)


def east(main, side):
    a, b = lanes(main, -1), lanes(side, -1)
    last = lane_of(main) == LANES - 1
    return jnp.where(last, b, a), jnp.where(last, a, b)


def west(main, side):
    a, b = lanes(main, 1), lanes(side, 1)
    first = lane_of(main) == 0
    return jnp.where(first, b, a), jnp.where(first, a, b)


def segments(layers):
    found, q = [], 0
    for field in range(2):
        k = 0
        while k < layers:
            n = min(layers - k, PER_TILE - q % PER_TILE)
            found.append((field, k, n, q // PER_TILE, q % PER_TILE))
            k, q = k + n, q + n
    return found


def kernel(
    nlon, nlat, tiles, centre,
    thick, ve, vn, cnt, height, te, tn,
    oe, on, oh, ome, omn,
    rows_e, rows_n, packed, from_east, from_west, corner, corner_count, inject,
    state, state_side, state_east, state_west,
    count, count_side, count_east, count_west,
    force, force_side, force_east, force_west,
    send, recv,
):
    layers, r, _ = ve.shape
    lon, lat = lax.axis_index("lon"), lax.axis_index("lat")
    offsets = [o for o in range(centre - tiles + 1, centre + 1) if o != 0]

    def device(dx, dy):
        return {"lon": lax.rem(lon + nlon + dx, nlon), "lat": lax.rem(lat + nlat + dy, nlat)}

    partners = [(1, 0), (-1, 0)] + [(0, o) for o in offsets]
    partners += [(dx, dy) for dx in (1, -1) for dy in (1, -1)]
    barrier = pltpu.get_barrier_semaphore()
    for dx, dy in partners:
        pl.semaphore_signal(barrier, inc=1, device_id=device(dx, dy), device_id_type=MESH)

    used = [0]
    started = []

    def push(src, dst, dx, dy):
        i = used[0]
        used[0] += 1
        c = pltpu.make_async_remote_copy(
            src_ref=src, dst_ref=dst, send_sem=send.at[i], recv_sem=recv.at[i],
            device_id=device(dx, dy), device_id_type=MESH)
        c.start()
        started.append(c)
        return c

    ntiles = packed.shape[0]
    for t in range(ntiles):
        acc = jnp.zeros((r, LANES), jnp.float32)
        for field, k0, n, tile, m0 in segments(layers):
            if tile != t:
                continue
            v = (ve, vn)[field]

            def put(i, acc, v=v, k0=k0, m0=m0):
                m = m0 + i
                x = pltpu.roll(v[k0 + i], GROUP * m + 2 - LANES * ((GROUP * m + 2) // LANES), 1)
                return jnp.where(lane_of(x) // GROUP == m, x, acc)

            acc = lax.fori_loop(0, n, put, acc, unroll=4)
        packed[t] = acc
    pl.semaphore_wait(barrier, len(partners))

    lon_v = [push(packed, from_west, 1, 0), push(packed, from_east, -1, 0)]
    diag = [(-1, -1, 0), (-1, 1, 1), (1, -1, 2), (1, 1, 3)]
    half = r // 2
    diag_v, diag_c = [], []
    for dx, dy, slot in diag:
        part = pl.ds(0, 8) if dy < 0 else pl.ds(r - 8, 8)
        diag_v.append(push(packed.at[:, part], corner.at[slot], dx, dy))
        diag_c.append(push(cnt.at[part], corner_count.at[slot], dx, dy))
    lon_c = [push(cnt, count_west, 1, 0), push(cnt, count_east, -1, 0)]
    lat_v = []
    for v, buf in ((ve, rows_e), (vn, rows_n)):
        lat_v.append(push(v.at[:, pl.ds(0, 2)], buf.at[:, pl.ds(0, 2)], 0, -1))
        lat_v.append(push(v.at[:, pl.ds(r - 2, 2)], buf.at[:, pl.ds(6, 2)], 0, 1))
    lat_c = [push(cnt, count.at[centre - o], 0, o) for o in offsets]
    fields = (height, te, tn)
    lon_s = []
    for i, f in enumerate(fields):
        lon_s.append(push(f, state_west.at[i], 1, 0))
        lon_s.append(push(f, state_east.at[i], -1, 0))
    lat_s = [push(f, state.at[centre - o, i], 0, o) for i, f in enumerate(fields) for o in offsets]
    count[centre] = cnt[...]
    for i, f in enumerate(fields):
        state[centre, i] = f[...]

    right = lax.broadcasted_iota(jnp.int32, (r, LANES), 1) < LANES // 2
    for c in lon_v + diag_v + diag_c + lon_c + lat_v + lat_c:
        c.wait_recv()

    low = lax.broadcasted_iota(jnp.int32, (8, LANES), 0) < 4

    def ring(x, north, south):
        return jnp.concatenate([x, jnp.where(low, north, south)], 0)

    c24 = ring(cnt[...], count[(centre + 1) % tiles, 0:8], count[(centre - 1) % tiles, r - 8:r])
    ce = ring(count_east[...], corner_count[0], corner_count[1])
    cw = ring(count_west[...], corner_count[2], corner_count[3])
    lane = lane_of(c24)
    face_e = jnp.minimum(c24, jnp.where(lane == LANES - 1, lanes(ce, -1), lanes(c24, -1)))
    face_n = jnp.minimum(c24, up(c24))

    def spread(x):
        x = jnp.where(lane < 2, x, 0)
        step = GROUP
        while step < LANES:
            x = x + lanes(x, step)
            step *= 2
        return x

    inner = spread(jnp.where(lane == 0, ce, lanes(cw, 2)))
    outer = spread(jnp.where(lane == 0, lanes(ce, -1), lanes(c24, 1)))
    edge_e = jnp.minimum(inner, outer)[:r]
    edge_n = jnp.minimum(inner, up(inner))[:r]
    slot16 = lax.broadcasted_iota(jnp.int32, (r, LANES), 1)
    place = slot16 % GROUP
    for t in range(ntiles):
        fe = ring(from_east[t], corner[0, t], corner[1, t])
        fw = ring(from_west[t], corner[2, t], corner[3, t])
        g = jnp.where(lane % GROUP == 0, lanes(fe, -2), fw)
        across = jnp.where(place == 0, lanes(fe[:r], -3), lanes(fw[:r], 1)) + lanes(packed[t], -1)
        q = t * PER_TILE + slot16 // GROUP
        k = jnp.where(q < layers, q, q - layers)
        wet = k < jnp.where(q < layers, edge_e, edge_n)
        e = jnp.where(wet, across + up(g)[:r] + down(g)[:r] - 4.0 * g[:r], 0.0)
        inject[t, 0:r] = jnp.where(place < 2, g[:r], lanes(e, 2))
        inject[t, r:r + 8] = g[r:]

    first, last = lane == 0, lane == LANES - 1
    first16, last16 = first[:r], last[:r]
    sums = []
    for field, (v, buf, face, out) in enumerate(((ve, rows_e, face_e, oe), (vn, rows_n, face_n, on))):

        def level(k, carry, field=field, v=v, buf=buf, face=face, out=out):
            total, column = carry
            q = field * layers + k
            t = q // PER_TILE
            m = q - t * PER_TILE
            own = v[k]
            x = jnp.concatenate([own, buf[k]], 0)
            j = inject[t]
            turn = LANES - 1 - GROUP * m
            turn = jnp.where(turn < 0, turn + LANES, turn)
            rim = pltpu.roll(j, turn, 1)
            rim2 = pltpu.roll(j[:r], jnp.where(turn < 2, turn + LANES - 2, turn - 2), 1)
            wet = k < face
            l1 = (jnp.where(last, rim, lanes(x, -1)) + jnp.where(first, rim, lanes(x, 1))
                  + up(x) + down(x) - 4.0 * x)
            l1 = jnp.where(wet, l1, 0.0)
            mid = l1[:r]
            l2 = (jnp.where(last16, rim2, lanes(mid, -1)) + jnp.where(first16, rim2, lanes(mid, 1))
                  + up(l1)[:r] + down(l1)[:r] - 4.0 * mid)
            tend = jnp.where(wet[:r], -VISCOSITY * l2, 0.0)
            after = own + tend
            out[k] = after
            return total + thick[k] * tend, column + thick[k] * after

        zero = jnp.zeros((r, LANES), jnp.float32)
        sums.append(lax.fori_loop(0, layers, level, (zero, zero), unroll=4))
    (sum_e, column_e), (sum_n, column_n) = sums
    force[centre, 0] = sum_e * (TIMESTEP / NSUB)
    force[centre, 1] = sum_n * (TIMESTEP / NSUB)
    lon_f = [push(force.at[centre], force_west, 1, 0), push(force.at[centre], force_east, -1, 0)]
    lat_f = [push(force.at[centre], force.at[centre - o], 0, o) for o in offsets]

    for c in lon_s:
        c.wait_recv()
    count_side[centre] = jnp.where(right, count_east[...], count_west[...])
    for i in range(3):
        state_side[centre, i] = jnp.where(right, state_east[i], state_west[i])
    side_c = [push(count_side.at[centre], count_side.at[centre - o], 0, o) for o in offsets]
    side_s = [push(state_side.at[centre], state_side.at[centre - o], 0, o) for o in offsets]

    for c in side_c + side_s + lat_s:
        c.wait_recv()
    span = tiles * r
    cm, cs = count[...].reshape(span, LANES), count_side[...].reshape(span, LANES)

    def deepen(k, carry):
        dm, ds = carry
        return jnp.where(k < cm, dm + thick[k], dm), jnp.where(k < cs, ds + thick[k], ds)

    zero = jnp.zeros((span, LANES), jnp.float32)
    dm, ds = lax.fori_loop(0, layers, deepen, (zero, zero), unroll=4)
    em, es = east(dm, ds)
    em, es = jnp.minimum(dm, em), jnp.minimum(ds, es)
    nm, ns = jnp.minimum(dm, up(dm)), jnp.minimum(ds, up(ds))

    def take(buf, i):
        return buf[:, i].reshape(span, LANES)

    def gate(depth, flux):
        return jnp.where(depth > 0, TIMESTEP * flux, 0.0)

    own = slice(centre * r, centre * r + r)
    depth_e, depth_n = em[own], nm[own]
    now = [take(state, 0), take(state_side, 0), gate(em, take(state, 1)), gate(es, take(state_side, 1)),
           gate(nm, take(state, 2)), gate(ns, take(state_side, 2))]
    square = TIMESTEP * TIMESTEP
    fixed = [square * em, square * es, square * nm, square * ns]

    for c in lon_f:
        c.wait_recv()
    for i in range(2):
        force_side[centre, i] = jnp.where(right, force_east[i], force_west[i])
    side_f = [push(force_side.at[centre], force_side.at[centre - o], 0, o) for o in offsets]
    for c in lat_f + side_f:
        c.wait_recv()
    fixed += [take(force, 0), take(force_side, 0), take(force, 1), take(force_side, 1)]

    zero = jnp.zeros((r, LANES), jnp.float32)
    totals = (zero, zero)
    plan = [(NSUB, span, 0)]
    if tiles >= 3:
        plan = [(NSUB - 16, span, 0), (8, 3 * r, (centre - 1) * r), (8, 2 * r, centre * r - half)]
    base = 0
    for steps, size, start in plan:
        cut = slice(start - base, start - base + size)
        now = [x[cut] for x in now]
        fixed = [x[cut] for x in fixed]
        base = start
        mine = slice(centre * r - base, centre * r - base + r)
        aem, aes, anm, ans, bem, bes, bnm, bns = fixed

        def step(_, carry, mine=mine, aem=aem, aes=aes, anm=anm, ans=ans, bem=bem, bes=bes, bnm=bnm, bns=bns):
            hm, hs, xm, xs, ym, ys, tot_e, tot_n = carry
            wm, ws = west(xm, xs)
            hm = hm - ((xm - wm) + (ym - down(ym)))
            hs = hs - ((xs - ws) + (ys - down(ys)))
            gm, gs = east(hm, hs)
            xm = xm - aem * (gm - hm) + bem
            xs = xs - aes * (gs - hs) + bes
            ym = ym - anm * (up(hm) - hm) + bnm
            ys = ys - ans * (up(hs) - hs) + bns
            return hm, hs, xm, xs, ym, ys, tot_e + xm[mine], tot_n + ym[mine]

        *now, tot_e, tot_n = lax.fori_loop(0, steps, step, (*now, *totals))
        totals = (tot_e, tot_n)
    oh[...] = now[0][mine]
    mean_e = totals[0] / (NSUB * TIMESTEP)
    mean_n = totals[1] / (NSUB * TIMESTEP)
    ome[...] = mean_e
    omn[...] = mean_n
    one = jnp.ones((r, LANES), jnp.float32)
    shift_e = (mean_e - column_e) / (depth_e + jnp.where(depth_e > 0, 0.0, one))
    shift_n = (mean_n - column_n) / (depth_n + jnp.where(depth_n > 0, 0.0, one))
    own_e, own_n = face_e[:r], face_n[:r]

    def finish(k, _):
        oe[k] = jnp.where(k < own_e, oe[k] + shift_e, 0.0)
        on[k] = jnp.where(k < own_n, on[k] + shift_n, 0.0)
        return 0

    lax.fori_loop(0, layers, finish, 0, unroll=4)
    for c in started:
        c.wait_send()


def solution(mesh):
    nlon, nlat = mesh.shape["lon"], mesh.shape["lat"]

    def shards(ve, vn, cnt, height, te, tn, thick):
        layers, r, width = ve.shape
        reach = -(-NSUB // r)
        tiles = min(nlat, 2 * reach + 1)
        centre = tiles // 2
        ntiles = -(-2 * layers // PER_TILE)
        f32, i32 = jnp.float32, jnp.int32
        tile = (r, width)
        vm = pltpu.VMEM
        vspec = pl.BlockSpec(memory_space=pltpu.VMEM)
        copies = 2 + 8 + 2 + 4 + 6 + 2 + 8 * (tiles - 1)
        return pl.pallas_call(
            functools.partial(kernel, nlon, nlat, tiles, centre),
            out_shape=(
                jax.ShapeDtypeStruct(ve.shape, f32),
                jax.ShapeDtypeStruct(ve.shape, f32),
                jax.ShapeDtypeStruct(tile, f32),
                jax.ShapeDtypeStruct(tile, f32),
                jax.ShapeDtypeStruct(tile, f32),
            ),
            in_specs=[pl.BlockSpec(memory_space=pltpu.SMEM)] + [vspec] * 6,
            out_specs=[vspec] * 5,
            scratch_shapes=[
                vm((layers, 8, width), f32),
                vm((layers, 8, width), f32),
                vm((ntiles, *tile), f32),
                vm((ntiles, *tile), f32),
                vm((ntiles, *tile), f32),
                vm((4, ntiles, 8, width), f32),
                vm((4, 8, width), i32),
                vm((ntiles, r + 8, width), f32),
                vm((tiles, 3, *tile), f32),
                vm((tiles, 3, *tile), f32),
                vm((3, *tile), f32),
                vm((3, *tile), f32),
                vm((tiles, *tile), i32),
                vm((tiles, *tile), i32),
                vm(tile, i32),
                vm(tile, i32),
                vm((tiles, 2, *tile), f32),
                vm((tiles, 2, *tile), f32),
                vm((2, *tile), f32),
                vm((2, *tile), f32),
                pltpu.SemaphoreType.DMA((copies,)),
                pltpu.SemaphoreType.DMA((copies,)),
            ],
            compiler_params=pltpu.CompilerParams(collective_id=0, has_side_effects=True),
        )(thick, ve, vn, cnt, height, te, tn)

    level = P(None, "lat", "lon")
    flat = P("lat", "lon")
    return jax.shard_map(
        shards,
        mesh=mesh,
        in_specs=(level, level, flat, flat, flat, flat, P()),
        out_specs=(level, level, flat, flat, flat),
        check_vma=False,
    )
```

time: 116 us -> 37 us (0.32)
  waiting for transfers between devices: 63.5 us -> 0 us
  Pallas kernels: 0 us -> 31.5 us
  starting transfers between devices: 24.7 us -> 0 us
  other arithmetic: 17.9 us -> 0 us
  local copies, waits for them, and re-layouts: 7.23 us -> 4.5 us
  loops' own time: 1.27 us -> 0 us
    ppermute x32 -> x0, waiting for transfers between devices: 63.5 us -> none  [the longest x16 39.5 us: padded_2(): before = lax.ppermute(last, axis, up)]
    pallas_call x0 -> x1, Pallas kernels: none -> 31.5 us  [shards(): pl.pallas_call(functools.partial(kernel, nlon, nlat, tiles, centre), out_...]
    ppermute x32 -> x0, starting transfers between devices: 24.7 us -> none  [the longest x16 18.1 us: padded_2(): before = lax.ppermute(last, axis, up)]
    slice x203 -> x0, local copies, waits for them, and re-layouts: 6.37 us -> none  [the longest x60 2.31 us: substep(): jnp.roll(height, -1, -1) - height]
    mul x11 -> x0, other arithmetic: 4.46 us -> none  [the longest x1 1.61 us: shards(): first_north = wide_north * inner_laplace(padded[layers:2 * layers])]
    unnamed x14 -> x13, local copies, waits for them, and re-layouts: 0.04 us -> 4.5 us
    concatenate x17 -> x0, other arithmetic: 3.86 us -> none  [the longest x16 2.75 us: padded_2(): x = jnp.concatenate([before, x, after], axis=dim)]
    add x36 -> x0, other arithmetic: 3.13 us -> none  [the longest x24 2.03 us: substep(): flux_east - timestep * depth_east * (jnp.roll(height, -1, -1) - height)]
  transfers between devices with their start and end apart: 32 -> 0, of which waited for: 32 -> 0; matrix products, arithmetic and copies ran while one was open for 1% -> 0% of each run, Pallas kernels for 0% -> 0%
where the time goes in v1:
time: 37 us; the launch traced here: 36.7 us
  Pallas kernels  31.5 us (85%)
  local copies, waits for them, and re-layouts  4.5 us (12%)
  between operations  0.66 us (2%)
    pallas_call x1, Pallas kernels, shards(): pl.pallas_call(functools.partial(kernel, nlon, nlat, tiles, centre), out_...  31.5 us
    unnamed x13, local copies, waits for them, and re-layouts  4.5 us

profile of v1, /device:TPU:0, one launch (start us, length us, event | category | flops | bytes accessed | tf_op | source)
XLA Modules:
  0.0 36.7 jit_solution(5016980060406189229)
XLA Ops:
  0.6 31.5 %shard_map.110 = (f32[40,16,128]{2,1,0:T(8,128)}, f32[40,16,128]{2,1,0:T(8,128)}, f32[16,128]{1,0:T(8,128)}, f32[16,128]{1,0:T(8,128)}, f32[16,128]{1,0:T(8,128)}) custom-call(f32[40]{0:T(128)} %thick.1, f32[40,16,128]{2,1,0:T(8,128)} %ve.1, f32[40,16,128]{2,1,0:T(8,128)} %vn.1, s32[16,128]{1,0:T(8,128)} %cnt.1, f32[16,128]{1,0:T(8,128)} %height.1, ...), custom_call_target="tpu_custom_call" | custom-call | tf_op jit(solution)/shard_map/pallas_call | solution.py:325
  32.2 0.0 copy-start
  32.2 1.8 %copy.17 = f32[40,16,128]{2,1,0:T(8,128)} copy(f32[40,16,128]{2,1,0:T(8,128)} %get-tuple-element.10) | data formatting | bytes 655360
  34.0 0.0 copy-done
  34.0 0.0 copy-start.3
  34.0 0.7 %copy.18 = f32[40,16,128]{2,1,0:T(8,128)} copy(f32[40,16,128]{2,1,0:T(8,128)S(1)} %copy-done) | data formatting | bytes 655360
  34.7 0.0 copy-done.3
  34.7 0.0 copy-start.2
  34.7 0.6 %copy.19 = f32[16,128]{1,0:T(8,128)} copy(f32[16,128]{1,0:T(8,128)S(1)} %copy-done.3) | data formatting | bytes 16384
  35.3 0.1 copy-done.2
  35.4 0.0 copy-start.1
  35.4 0.6 %copy.20 = f32[16,128]{1,0:T(8,128)} copy(f32[16,128]{1,0:T(8,128)S(1)} %copy-done.2) | data formatting | bytes 16384
  36.0 0.1 copy-done.1
  36.1 0.6 %copy.21 = f32[16,128]{1,0:T(8,128)} copy(f32[16,128]{1,0:T(8,128)S(1)} %copy-done.1) | data formatting | bytes 16384
Async XLA Ops:
  32.2 1.8 %copy-start = (f32[40,16,128]{2,1,0:T(8,128)S(1)}, f32[40,16,128]{2,1,0:T(8,128)}, u32[]{:S(2)}) copy-start(f32[40,16,128]{2,1,0:T(8,128)} %get-tuple-element.11) | copy-start | bytes 983044
  34.0 0.7 %copy-start.3 = (f32[16,128]{1,0:T(8,128)S(1)}, f32[16,128]{1,0:T(8,128)}, u32[]{:S(2)}) copy-start(f32[16,128]{1,0:T(8,128)} %get-tuple-element.12) | copy-start | bytes 24580
  34.7 0.7 %copy-start.2 = (f32[16,128]{1,0:T(8,128)S(1)}, f32[16,128]{1,0:T(8,128)}, u32[]{:S(2)}) copy-start(f32[16,128]{1,0:T(8,128)} %get-tuple-element.13) | copy-start | bytes 24580
  35.4 0.7 %copy-start.1 = (f32[16,128]{1,0:T(8,128)S(1)}, f32[16,128]{1,0:T(8,128)}, u32[]{:S(2)}) copy-start(f32[16,128]{1,0:T(8,128)} %get-tuple-element.14) | copy-start | bytes 24580

commit v2 on v1

--- a/solution.py
+++ b/solution.py
@@ -61,8 +61,9 @@
 
 def kernel(
     nlon, nlat, tiles, centre,
-    thick, ve, vn, cnt, height, te, tn,
-    oe, on, oh, ome, omn,
+    thick_hbm, ve_hbm, vn_hbm, cnt_hbm, height_hbm, te_hbm, tn_hbm,
+    oe, on, small,
+    thick, ve, vn, cnt, height, te, tn, loads,
     rows_e, rows_n, packed, from_east, from_west, corner, corner_count, inject,
     state, state_side, state_east, state_west,
     count, count_side, count_east, count_west,
@@ -82,6 +83,14 @@
     for dx, dy in partners:
         pl.semaphore_signal(barrier, inc=1, device_id=device(dx, dy), device_id_type=MESH)
 
+    fetched = []
+    for i, (far, near) in enumerate((
+        (ve_hbm, ve), (vn_hbm, vn), (cnt_hbm, cnt), (height_hbm, height), (te_hbm, te), (tn_hbm, tn),
+        (thick_hbm, thick),
+    )):
+        fetched.append(pltpu.make_async_copy(far, near, loads.at[i]))
+        fetched[-1].start()
+
     used = [0]
     started = []
 
@@ -94,6 +103,9 @@
         c.start()
         started.append(c)
         return c
+
+    for c in fetched:
+        c.wait()
 
     ntiles = packed.shape[0]
     for t in range(ntiles):
@@ -288,24 +300,34 @@
 
         *now, tot_e, tot_n = lax.fori_loop(0, steps, step, (*now, *totals))
         totals = (tot_e, tot_n)
-    oh[...] = now[0][mine]
     mean_e = totals[0] / (NSUB * TIMESTEP)
     mean_n = totals[1] / (NSUB * TIMESTEP)
-    ome[...] = mean_e
-    omn[...] = mean_n
     one = jnp.ones((r, LANES), jnp.float32)
-    shift_e = (mean_e - column_e) / (depth_e + jnp.where(depth_e > 0, 0.0, one))
-    shift_n = (mean_n - column_n) / (depth_n + jnp.where(depth_n > 0, 0.0, one))
-    own_e, own_n = face_e[:r], face_n[:r]
-
-    def finish(k, _):
-        oe[k] = jnp.where(k < own_e, oe[k] + shift_e, 0.0)
-        on[k] = jnp.where(k < own_n, on[k] + shift_n, 0.0)
-        return 0
-
-    lax.fori_loop(0, layers, finish, 0, unroll=4)
+    small[0] = now[0][mine]
+    small[1] = mean_e
+    small[2] = mean_n
+    small[3] = (mean_e - column_e) / (depth_e + jnp.where(depth_e > 0, 0.0, one))
+    small[4] = (mean_n - column_n) / (depth_n + jnp.where(depth_n > 0, 0.0, one))
+    small[5] = face_e[:r].astype(jnp.float32)
+    small[6] = face_n[:r].astype(jnp.float32)
     for c in started:
         c.wait_send()
+
+
+def finish(after_e, after_n, small, oe, on, oh, ome, omn):
+    oh[...] = small[0]
+    ome[...] = small[1]
+    omn[...] = small[2]
+    face_e, face_n = small[5], small[6]
+    shift_e, shift_n = small[3], small[4]
+
+    def level(k, _):
+        depth = k.astype(jnp.float32)
+        oe[k] = jnp.where(depth < face_e, after_e[k] + shift_e, 0.0)
+        on[k] = jnp.where(depth < face_n, after_n[k] + shift_n, 0.0)
+        return 0
+
+    lax.fori_loop(0, after_e.shape[0], level, 0, unroll=4)
 
 
 def solution(mesh):
@@ -322,18 +344,24 @@
         vm = pltpu.VMEM
         vspec = pl.BlockSpec(memory_space=pltpu.VMEM)
         copies = 2 + 8 + 2 + 4 + 6 + 2 + 8 * (tiles - 1)
-        return pl.pallas_call(
+        after_e, after_n, small = pl.pallas_call(
             functools.partial(kernel, nlon, nlat, tiles, centre),
             out_shape=(
                 jax.ShapeDtypeStruct(ve.shape, f32),
                 jax.ShapeDtypeStruct(ve.shape, f32),
-                jax.ShapeDtypeStruct(tile, f32),
-                jax.ShapeDtypeStruct(tile, f32),
-                jax.ShapeDtypeStruct(tile, f32),
+                jax.ShapeDtypeStruct((7, *tile), f32),
             ),
-            in_specs=[pl.BlockSpec(memory_space=pltpu.SMEM)] + [vspec] * 6,
-            out_specs=[vspec] * 5,
+            in_specs=[pl.BlockSpec(memory_space=pltpu.HBM)] * 7,
+            out_specs=[vspec] * 3,
             scratch_shapes=[
+                pltpu.SMEM((layers,), f32),
+                vm(ve.shape, f32),
+                vm(ve.shape, f32),
+                vm(tile, i32),
+                vm(tile, f32),
+                vm(tile, f32),
+                vm(tile, f32),
+                pltpu.SemaphoreType.DMA((7,)),
                 vm((layers, 8, width), f32),
                 vm((layers, 8, width), f32),
                 vm((ntiles, *tile), f32),
@@ -357,8 +385,18 @@
                 pltpu.SemaphoreType.DMA((copies,)),
                 pltpu.SemaphoreType.DMA((copies,)),
             ],
-            compiler_params=pltpu.CompilerParams(collective_id=0, has_side_effects=True),
-        )(thick, ve, vn, cnt, height, te, tn)
+            compiler_params=pltpu.CompilerParams(
+                collective_id=0, has_side_effects=True, vmem_limit_bytes=16 << 20),
+        )(*[pltpu.with_memory_space_constraint(x, pltpu.HBM) for x in (thick, ve, vn, cnt, height, te, tn)])
+        out = jax.ShapeDtypeStruct(tile, f32)
+        levels = jax.ShapeDtypeStruct(ve.shape, f32)
+        return pl.pallas_call(
+            finish,
+            out_shape=(levels, levels, out, out, out),
+            in_specs=[vspec] * 3,
+            out_specs=[vspec] * 5,
+            compiler_params=pltpu.CompilerParams(vmem_limit_bytes=16 << 20),
+        )(after_e, after_n, small)
 
     level = P(None, "lat", "lon")
     flat = P("lat", "lon")

time: 37 us -> 31.3 us (0.85)
  local copies, waits for them, and re-layouts: 4.5 us -> 0 us
  Pallas kernels: 31.5 us -> 30.5 us
    unnamed x13 -> x0, local copies, waits for them, and re-layouts: 4.5 us -> none
    pallas_call x1, Pallas kernels: 31.5 us -> 29.6 us  [shards(): pl.pallas_call(functools.partial(kernel, nlon, nlat, tiles, centre), out_...]
    pallas_call x0 -> x1, Pallas kernels: none -> 0.95 us  [shards(): pl.pallas_call(finish, out_shape=(levels, levels, out, out, out), in_spec...]
where the time goes in v2:
time: 31.3 us; the launch traced here: 31.1 us
  Pallas kernels  30.5 us (97%)
  between operations  0.64 us (2%)
    pallas_call x1, Pallas kernels, shards(): pl.pallas_call(functools.partial(kernel, nlon, nlat, tiles, centre), out_...  29.6 us
    pallas_call x1, Pallas kernels, shards(): pl.pallas_call(finish, out_shape=(levels, levels, out, out, out), in_spec...  0.95 us

profile of v2, /device:TPU:0, one launch (start us, length us, event | category | flops | bytes accessed | tf_op | source)
XLA Modules:
  0.0 31.1 jit_solution(14488717811130395853)
XLA Ops:
  0.6 29.6 %shard_map.110 = (f32[40,16,128]{2,1,0:T(8,128)S(1)}, f32[40,16,128]{2,1,0:T(8,128)S(1)}, f32[7,16,128]{2,1,0:T(8,128)S(1)}) custom-call(f32[40]{0:T(128)} %thick_hbm.1, f32[40,16,128]{2,1,0:T(8,128)} %ve_hbm.1, f32[40,16,128]{2,1,0:T(8,128)} %vn_hbm.1, s32[16,128]{1,0:T(8,128)} %cnt_hbm.1, f32[16,128]{1,0:T(8,128)} %height_hbm.1, f32[16,128]{1,0:T(8,128)} %te_hbm.1, ...), custom_call_target="tpu_custom_call" | custom-call | tf_op jit(solution)/shard_map/pallas_call | solution.py:347
  30.2 0.9 %shard_map.111 = (f32[40,16,128]{2,1,0:T(8,128)}, f32[40,16,128]{2,1,0:T(8,128)}, f32[16,128]{1,0:T(8,128)}, f32[16,128]{1,0:T(8,128)}, f32[16,128]{1,0:T(8,128)}) custom-call(f32[40,16,128]{2,1,0:T(8,128)S(1)} %get-tuple-element.8.after_e, f32[40,16,128]{2,1,0:T(8,128)S(1)} %get-tuple-element.9.after_n, f32[7,16,128]{2,1,0:T(8,128)S(1)} %get-tuple-element.10.small), custom_call_target="tpu_custom_call" | custom-call | tf_op jit(solution)/shard_map/pallas_call | solution.py:393

commit v3 on v2

--- a/solution.py
+++ b/solution.py
@@ -13,6 +13,7 @@
 LANES = 128
 GROUP = 4
 PER_TILE = LANES // GROUP
+UNROLL = 8
 MESH = pl.DeviceIdType.MESH
 
 
@@ -67,7 +68,7 @@
     rows_e, rows_n, packed, from_east, from_west, corner, corner_count, inject,
     state, state_side, state_east, state_west,
     count, count_side, count_east, count_west,
-    force, force_side, force_east, force_west,
+    force, force_out, force_east, force_west,
     send, recv,
 ):
     layers, r, _ = ve.shape
@@ -78,7 +79,7 @@
         return {"lon": lax.rem(lon + nlon + dx, nlon), "lat": lax.rem(lat + nlat + dy, nlat)}
 
     partners = [(1, 0), (-1, 0)] + [(0, o) for o in offsets]
-    partners += [(dx, dy) for dx in (1, -1) for dy in (1, -1)]
+    partners += [(dx, o) for dx in (1, -1) for o in offsets]
     barrier = pltpu.get_barrier_semaphore()
     for dx, dy in partners:
         pl.semaphore_signal(barrier, inc=1, device_id=device(dx, dy), device_id_type=MESH)
@@ -192,7 +193,7 @@
 
     first, last = lane == 0, lane == LANES - 1
     first16, last16 = first[:r], last[:r]
-    sums = []
+    sums, side_c, side_s = [], [], []
     for field, (v, buf, face, out) in enumerate(((ve, rows_e, face_e, oe), (vn, rows_n, face_n, on))):
 
         def level(k, carry, field=field, v=v, buf=buf, face=face, out=out):
@@ -220,20 +221,29 @@
             return total + thick[k] * tend, column + thick[k] * after
 
         zero = jnp.zeros((r, LANES), jnp.float32)
-        sums.append(lax.fori_loop(0, layers, level, (zero, zero), unroll=4))
+        sums.append(lax.fori_loop(0, layers, level, (zero, zero), unroll=UNROLL))
+        if field == 0:
+            for c in lon_s:
+                c.wait_recv()
+            count_side[centre] = jnp.where(right, count_east[...], count_west[...])
+            for i in range(3):
+                state_side[centre, i] = jnp.where(right, state_east[i], state_west[i])
+            side_c = [push(count_side.at[centre], count_side.at[centre - o], 0, o) for o in offsets]
+            side_s = [push(state_side.at[centre], state_side.at[centre - o], 0, o) for o in offsets]
     (sum_e, column_e), (sum_n, column_n) = sums
-    force[centre, 0] = sum_e * (TIMESTEP / NSUB)
-    force[centre, 1] = sum_n * (TIMESTEP / NSUB)
-    lon_f = [push(force.at[centre], force_west, 1, 0), push(force.at[centre], force_east, -1, 0)]
+    sum_e, sum_n = sum_e * (TIMESTEP / NSUB), sum_n * (TIMESTEP / NSUB)
+    force[centre, 0] = sum_e
+    force[centre, 1] = sum_n
+    quarter, middle = LANES // 4, LANES // 2
+    out = jnp.where(slot16 >= LANES - quarter, sum_e, lanes(sum_n, -quarter))
+    force_out[0] = jnp.where(right[:8], lanes(out[:8], middle), out[8:])
+    out = jnp.where(slot16 < quarter, sum_e, lanes(sum_n, quarter))
+    force_out[1] = jnp.where(right[:8], out[:8], lanes(out[8:], middle))
+    side_f = []
+    for o in [0] + offsets:
+        side_f.append(push(force_out.at[0], force_west.at[centre - o], 1, o))
+        side_f.append(push(force_out.at[1], force_east.at[centre - o], -1, o))
     lat_f = [push(force.at[centre], force.at[centre - o], 0, o) for o in offsets]
-
-    for c in lon_s:
-        c.wait_recv()
-    count_side[centre] = jnp.where(right, count_east[...], count_west[...])
-    for i in range(3):
-        state_side[centre, i] = jnp.where(right, state_east[i], state_west[i])
-    side_c = [push(count_side.at[centre], count_side.at[centre - o], 0, o) for o in offsets]
-    side_s = [push(state_side.at[centre], state_side.at[centre - o], 0, o) for o in offsets]
 
     for c in side_c + side_s + lat_s:
         c.wait_recv()
@@ -258,52 +268,68 @@
 
     own = slice(centre * r, centre * r + r)
     depth_e, depth_n = em[own], nm[own]
-    now = [take(state, 0), take(state_side, 0), gate(em, take(state, 1)), gate(es, take(state_side, 1)),
-           gate(nm, take(state, 2)), gate(ns, take(state_side, 2))]
+    xm, xs = gate(em, take(state, 1)), gate(es, take(state_side, 1))
+    ym, ys = gate(nm, take(state, 2)), gate(ns, take(state_side, 2))
+
+    def divergence(xm, xs, ym, ys):
+        wm, ws = west(xm, xs)
+        return (xm - wm) + (ym - down(ym)), (xs - ws) + (ys - down(ys))
+
     square = TIMESTEP * TIMESTEP
-    fixed = [square * em, square * es, square * nm, square * ns]
-
-    for c in lon_f:
-        c.wait_recv()
-    for i in range(2):
-        force_side[centre, i] = jnp.where(right, force_east[i], force_west[i])
-    side_f = [push(force_side.at[centre], force_side.at[centre - o], 0, o) for o in offsets]
+    aem, aes, anm, ans = square * em, square * es, square * nm, square * ns
+    awm, aws = west(aem, aes)
+    asm, ass = down(anm), down(ans)
+    start_e, start_n = xm[own], ym[own]
+    now = [take(state, 0), take(state_side, 0), *divergence(xm, xs, ym, ys)]
+    fixed = [aem, aes, awm, aws, anm, ans, asm, ass, aem + awm + anm + asm, aes + aws + ans + ass]
+
     for c in lat_f + side_f:
         c.wait_recv()
-    fixed += [take(force, 0), take(force_side, 0), take(force, 1), take(force_side, 1)]
-
-    zero = jnp.zeros((r, LANES), jnp.float32)
-    totals = (zero, zero)
+    fe = jnp.concatenate([x for s in range(tiles) for x in (force_east[s], lanes(force_east[s], middle))], 0)
+    fw = jnp.concatenate([x for s in range(tiles) for x in (lanes(force_west[s], middle), force_west[s])], 0)
+    near = lane_of(fe) < middle
+    fm_e, fm_n = take(force, 0), take(force, 1)
+    fs_e = jnp.where(near, fe, fw)
+    fs_n = jnp.where(near, lanes(fe, -quarter), lanes(fw, quarter))
+    fixed += divergence(fm_e, fs_e, fm_n, fs_n)
+
     plan = [(NSUB, span, 0)]
     if tiles >= 3:
         plan = [(NSUB - 16, span, 0), (8, 3 * r, (centre - 1) * r), (8, 2 * r, centre * r - half)]
-    base = 0
-    for steps, size, start in plan:
-        cut = slice(start - base, start - base + size)
+    size, low_row = plan[-1][1], plan[-1][2]
+    weighted = (jnp.zeros((size, LANES), jnp.float32), jnp.zeros((size, LANES), jnp.float32))
+    base, done = 0, 0
+    for steps, rows, start in plan:
+        cut = slice(start - base, start - base + rows)
         now = [x[cut] for x in now]
         fixed = [x[cut] for x in fixed]
         base = start
-        mine = slice(centre * r - base, centre * r - base + r)
-        aem, aes, anm, ans, bem, bes, bnm, bns = fixed
-
-        def step(_, carry, mine=mine, aem=aem, aes=aes, anm=anm, ans=ans, bem=bem, bes=bes, bnm=bnm, bns=bns):
-            hm, hs, xm, xs, ym, ys, tot_e, tot_n = carry
-            wm, ws = west(xm, xs)
-            hm = hm - ((xm - wm) + (ym - down(ym)))
-            hs = hs - ((xs - ws) + (ys - down(ys)))
-            gm, gs = east(hm, hs)
-            xm = xm - aem * (gm - hm) + bem
-            xs = xs - aes * (gs - hs) + bes
-            ym = ym - anm * (up(hm) - hm) + bnm
-            ys = ys - ans * (up(hs) - hs) + bns
-            return hm, hs, xm, xs, ym, ys, tot_e + xm[mine], tot_n + ym[mine]
-
-        *now, tot_e, tot_n = lax.fori_loop(0, steps, step, (*now, *totals))
-        totals = (tot_e, tot_n)
-    mean_e = totals[0] / (NSUB * TIMESTEP)
-    mean_n = totals[1] / (NSUB * TIMESTEP)
+        mine = slice(low_row - base, low_row - base + size)
+
+        def step(i, carry, mine=mine, fixed=fixed, done=done):
+            hm, hs, zm, zs, um, us = carry
+            aem, aes, awm, aws, anm, ans, asm, ass, acm, acs, dm, ds = fixed
+            hm, hs = hm - zm, hs - zs
+            (gm, gs), (wm, ws) = east(hm, hs), west(hm, hs)
+            zm = zm + ((acm * hm + dm) - (aem * gm + awm * wm) - (anm * up(hm) + asm * down(hm)))
+            zs = zs + ((acs * hs + ds) - (aes * gs + aws * ws) - (ans * up(hs) + ass * down(hs)))
+            weight = (NSUB - done - i).astype(jnp.float32)
+            return hm, hs, zm, zs, um + weight * hm[mine], us + weight * hs[mine]
+
+        *now, um, us = lax.fori_loop(0, steps, step, (*now, *weighted))
+        weighted = (um, us)
+        done += steps
+    um, us = weighted
+    gm, _ = east(um, us)
+    mine = slice(centre * r - base, centre * r - base + r)
+    final = now[0][mine]
+    ramp = NSUB * (NSUB + 1) / 2
+    total_e = NSUB * start_e - square * depth_e * (gm - um)[mine] + ramp * sum_e
+    total_n = NSUB * start_n - square * depth_n * (up(um) - um)[mine] + ramp * sum_n
+    mean_e = total_e / (NSUB * TIMESTEP)
+    mean_n = total_n / (NSUB * TIMESTEP)
     one = jnp.ones((r, LANES), jnp.float32)
-    small[0] = now[0][mine]
+    small[0] = final
     small[1] = mean_e
     small[2] = mean_n
     small[3] = (mean_e - column_e) / (depth_e + jnp.where(depth_e > 0, 0.0, one))
@@ -343,7 +369,7 @@
         tile = (r, width)
         vm = pltpu.VMEM
         vspec = pl.BlockSpec(memory_space=pltpu.VMEM)
-        copies = 2 + 8 + 2 + 4 + 6 + 2 + 8 * (tiles - 1)
+        copies = 2 + 8 + 2 + 4 + 6 + 2 + 9 * (tiles - 1)
         after_e, after_n, small = pl.pallas_call(
             functools.partial(kernel, nlon, nlat, tiles, centre),
             out_shape=(
@@ -379,9 +405,9 @@
                 vm(tile, i32),
                 vm(tile, i32),
                 vm((tiles, 2, *tile), f32),
-                vm((tiles, 2, *tile), f32),
-                vm((2, *tile), f32),
-                vm((2, *tile), f32),
+                vm((2, 8, width), f32),
+                vm((tiles, 8, width), f32),
+                vm((tiles, 8, width), f32),
                 pltpu.SemaphoreType.DMA((copies,)),
                 pltpu.SemaphoreType.DMA((copies,)),
             ],

time: 31.3 us -> 25.3 us (0.81)
  Pallas kernels: 30.5 us -> 24.5 us
    pallas_call x1, Pallas kernels: 29.6 us -> 23.6 us  [shards(): pl.pallas_call(functools.partial(kernel, nlon, nlat, tiles, centre), out_...]
where the time goes in v3:
time: 25.3 us; the launch traced here: 25.2 us
  Pallas kernels  24.5 us (97%)
  between operations  0.64 us (3%)
    pallas_call x1, Pallas kernels, shards(): pl.pallas_call(functools.partial(kernel, nlon, nlat, tiles, centre), out_...  23.6 us
    pallas_call x1, Pallas kernels, shards(): pl.pallas_call(finish, out_shape=(levels, levels, out, out, out), in_spec...  0.95 us

profile of v3, /device:TPU:0, one launch (start us, length us, event | category | flops | bytes accessed | tf_op | source)
XLA Modules:
  0.0 25.2 jit_solution(10957953249424631542)
XLA Ops:
  0.6 23.6 %shard_map.110 = (f32[40,16,128]{2,1,0:T(8,128)S(1)}, f32[40,16,128]{2,1,0:T(8,128)S(1)}, f32[7,16,128]{2,1,0:T(8,128)S(1)}) custom-call(f32[40]{0:T(128)} %thick_hbm.1, f32[40,16,128]{2,1,0:T(8,128)} %ve_hbm.1, f32[40,16,128]{2,1,0:T(8,128)} %vn_hbm.1, s32[16,128]{1,0:T(8,128)} %cnt_hbm.1, f32[16,128]{1,0:T(8,128)} %height_hbm.1, f32[16,128]{1,0:T(8,128)} %te_hbm.1, ...), custom_call_target="tpu_custom_call" | custom-call | tf_op jit(solution)/shard_map/pallas_call | solution.py:373
  24.2 0.9 %shard_map.111 = (f32[40,16,128]{2,1,0:T(8,128)}, f32[40,16,128]{2,1,0:T(8,128)}, f32[16,128]{1,0:T(8,128)}, f32[16,128]{1,0:T(8,128)}, f32[16,128]{1,0:T(8,128)}) custom-call(f32[40,16,128]{2,1,0:T(8,128)S(1)} %get-tuple-element.8.after_e, f32[40,16,128]{2,1,0:T(8,128)S(1)} %get-tuple-element.9.after_n, f32[7,16,128]{2,1,0:T(8,128)S(1)} %get-tuple-element.10.small), custom_call_target="tpu_custom_call" | custom-call | tf_op jit(solution)/shard_map/pallas_call | solution.py:419

commit v4 on v3

--- a/solution.py
+++ b/solution.py
@@ -125,20 +125,21 @@
         packed[t] = acc
     pl.semaphore_wait(barrier, len(partners))
 
-    lon_v = [push(packed, from_west, 1, 0), push(packed, from_east, -1, 0)]
+    lon_c = [push(cnt, count_west, 1, 0), push(cnt, count_east, -1, 0)]
+    diag_c, diag_v, lat_v = [], [], []
     diag = [(-1, -1, 0), (-1, 1, 1), (1, -1, 2), (1, 1, 3)]
     half = r // 2
-    diag_v, diag_c = [], []
+    for dx, dy, slot in diag:
+        part = pl.ds(0, 8) if dy < 0 else pl.ds(r - 8, 8)
+        diag_c.append(push(cnt.at[part], corner_count.at[slot], dx, dy))
+    lat_c = [push(cnt, count.at[centre - o], 0, o) for o in offsets]
     for dx, dy, slot in diag:
         part = pl.ds(0, 8) if dy < 0 else pl.ds(r - 8, 8)
         diag_v.append(push(packed.at[:, part], corner.at[slot], dx, dy))
-        diag_c.append(push(cnt.at[part], corner_count.at[slot], dx, dy))
-    lon_c = [push(cnt, count_west, 1, 0), push(cnt, count_east, -1, 0)]
-    lat_v = []
+    lon_v = [push(packed, from_west, 1, 0), push(packed, from_east, -1, 0)]
     for v, buf in ((ve, rows_e), (vn, rows_n)):
         lat_v.append(push(v.at[:, pl.ds(0, 2)], buf.at[:, pl.ds(0, 2)], 0, -1))
         lat_v.append(push(v.at[:, pl.ds(r - 2, 2)], buf.at[:, pl.ds(6, 2)], 0, 1))
-    lat_c = [push(cnt, count.at[centre - o], 0, o) for o in offsets]
     fields = (height, te, tn)
     lon_s = []
     for i, f in enumerate(fields):
@@ -150,7 +151,7 @@
         state[centre, i] = f[...]
 
     right = lax.broadcasted_iota(jnp.int32, (r, LANES), 1) < LANES // 2
-    for c in lon_v + diag_v + diag_c + lon_c + lat_v + lat_c:
+    for c in lon_c + diag_c + lat_c:
         c.wait_recv()
 
     low = lax.broadcasted_iota(jnp.int32, (8, LANES), 0) < 4
@@ -179,6 +180,8 @@
     edge_n = jnp.minimum(inner, up(inner))[:r]
     slot16 = lax.broadcasted_iota(jnp.int32, (r, LANES), 1)
     place = slot16 % GROUP
+    for c in lon_v + diag_v:
+        c.wait_recv()
     for t in range(ntiles):
         fe = ring(from_east[t], corner[0, t], corner[1, t])
         fw = ring(from_west[t], corner[2, t], corner[3, t])
@@ -193,6 +196,8 @@
 
     first, last = lane == 0, lane == LANES - 1
     first16, last16 = first[:r], last[:r]
+    for c in lat_v:
+        c.wait_recv()
     sums, side_c, side_s = [], [], []
     for field, (v, buf, face, out) in enumerate(((ve, rows_e, face_e, oe), (vn, rows_n, face_n, on))):
 

time: 25.3 us -> 25 us (0.988)
  Pallas kernels: 24.5 us -> 24.2 us
    pallas_call x1, Pallas kernels: 23.6 us -> 23.2 us  [shards(): pl.pallas_call(functools.partial(kernel, nlon, nlat, tiles, centre), out_...]
where the time goes in v4:
time: 25 us; the launch traced here: 24.8 us
  Pallas kernels  24.2 us (97%)
  between operations  0.64 us (3%)
    pallas_call x1, Pallas kernels, shards(): pl.pallas_call(functools.partial(kernel, nlon, nlat, tiles, centre), out_...  23.2 us
    pallas_call x1, Pallas kernels, shards(): pl.pallas_call(finish, out_shape=(levels, levels, out, out, out), in_spec...  0.95 us

profile of v4, /device:TPU:0, one launch (start us, length us, event | category | flops | bytes accessed | tf_op | source)
XLA Modules:
  0.0 24.8 jit_solution(7967269387478994908)
XLA Ops:
  0.6 23.2 %shard_map.110 = (f32[40,16,128]{2,1,0:T(8,128)S(1)}, f32[40,16,128]{2,1,0:T(8,128)S(1)}, f32[7,16,128]{2,1,0:T(8,128)S(1)}) custom-call(f32[40]{0:T(128)} %thick_hbm.1, f32[40,16,128]{2,1,0:T(8,128)} %ve_hbm.1, f32[40,16,128]{2,1,0:T(8,128)} %vn_hbm.1, s32[16,128]{1,0:T(8,128)} %cnt_hbm.1, f32[16,128]{1,0:T(8,128)} %height_hbm.1, f32[16,128]{1,0:T(8,128)} %te_hbm.1, ...), custom_call_target="tpu_custom_call" | custom-call | tf_op jit(solution)/shard_map/pallas_call | solution.py:378
  23.9 0.9 %shard_map.111 = (f32[40,16,128]{2,1,0:T(8,128)}, f32[40,16,128]{2,1,0:T(8,128)}, f32[16,128]{1,0:T(8,128)}, f32[16,128]{1,0:T(8,128)}, f32[16,128]{1,0:T(8,128)}) custom-call(f32[40,16,128]{2,1,0:T(8,128)S(1)} %get-tuple-element.8.after_e, f32[40,16,128]{2,1,0:T(8,128)S(1)} %get-tuple-element.9.after_n, f32[7,16,128]{2,1,0:T(8,128)S(1)} %get-tuple-element.10.small), custom_call_target="tpu_custom_call" | custom-call | tf_op jit(solution)/shard_map/pallas_call | solution.py:424
